TPU v7x, 256 devices: a whole 4x4x8 slice. The times are simulated.
256 devices in a mesh: rows: 64 (over y, z, core), feat: 4 (over x).
Axes of the slice: x: 4, y: 4, z: 8, core: 2. Of those that a mesh axis runs over, the one named last changes fastest.
Arguments:
- cells: bfloat16 [8192, 80, 128], P('rows', 'feat'), may hold values from -19 to 19
- block_table: int32 [64], replicated, may hold values from 0 to 7, as said below
- row_live: int32 [8192], replicated, may hold values from 0 to 1, as said below
- row_train: int32 [8192], replicated, may hold values from 0 to 1, as said below
- feat_qkv: bfloat16 [128, 384], replicated, may hold values from -0.5 to 0.5
- feat_out: bfloat16 [128, 128], replicated, may hold values from -0.5 to 0.5
- item_qkv: bfloat16 [128, 384], replicated, may hold values from -0.5 to 0.5
- item_out: bfloat16 [128, 128], replicated, may hold values from -0.5 to 0.5
Outputs:
- layer_output: bfloat16 [8192, 80, 128], P(('rows', 'feat'))
Inputs may be any that keep to these rules, and one draw needn't show every extreme that they name: `block_table`: every table number appears in some block. `row_live`: every training row is live. `row_train`: each aligned group of 32 rows holds 1 to 4 training rows; some group holds exactly 4.
All inputs are finite; a program needn't handle non-finite values.
Results may differ from a plain program's by a relative error of at most 0.014.
Values may be sent and summed in bfloat16 or wider, within the bound.
A program may use at most 64 MiB of HBM per device.

v0:
```python
import jax
import jax.numpy as jnp
from jax import lax
from jax.sharding import PartitionSpec as P

HEADS = 4
HEAD_DIM = 32
KEEP = 4
TABLES = 8


EPSILON = 1e-05
MASKED = -1e30


def from_everyone(shard, axis):
    peers = lax.axis_size(axis)
    return lax.all_to_all(
        jnp.broadcast_to(shard[None], (peers, *shard.shape)), axis, 0, 0, tiled=True
    )


def of_everyone(shard, axis):
    everything = from_everyone(shard, axis)
    return jnp.sum(everything, axis=0)


def in_one(arrays, axis):
    vector, at, done = (jnp.concatenate([a.reshape(-1) for a in arrays]), 0, [])
    so_far = of_everyone(vector, axis)
    for a in arrays:
        done.append(so_far[at : at + a.size].reshape(a.shape))
        at += a.size
    return tuple(done)


def laid_out(parts, dim):
    lengths = list(parts.shape[1:])
    lengths[dim] *= parts.shape[0]
    return jnp.moveaxis(parts, 0, dim).reshape(lengths)


def gather_together(arrays, axis, dims):
    vector = jnp.concatenate([a.reshape(-1) for a in arrays])
    lines, at, done = (lax.all_gather(vector, axis), 0, [])
    for a, dim in zip(arrays, dims):
        parts = lines[:, at : at + a.size].reshape(-1, *a.shape)
        done.append(laid_out(parts, dim))
        at += a.size
    return tuple(done)


def compact_train(train_rows):
    positions = jnp.arange(train_rows.shape[-1], dtype=jnp.int32)
    ordinal = jnp.cumsum(train_rows, axis=-1) - 1
    slot_ids = jnp.arange(KEEP, dtype=jnp.int32)
    matched = (train_rows[..., None, :] == 1) & (ordinal[..., None, :] == slot_ids[:, None])
    return jnp.sum(jnp.where(matched, positions, 0), axis=-1)


def into_heads(tensor):
    return tensor.reshape(tensor.shape[:-1] + (HEADS, HEAD_DIM))


def attend_features(queries, key_part, value_part):
    row_count, query_feats = (queries.shape[0], queries.shape[1])
    blocks = max(1, row_count * query_feats // 1280)
    while row_count % blocks:
        blocks -= 1
    scaling = HEAD_DIM ** (-0.5)

    def attend_one_block(block_parts):
        block_query, block_key, block_value = block_parts
        scores = (
            jnp.einsum(
                "rqhd,rkhd->rhqk", block_query, block_key, preferred_element_type=jnp.float32
            )
            * scaling
        )
        shares = jax.nn.softmax(scores, axis=-1).astype(jnp.bfloat16)
        return jnp.einsum(
            "rhqk,rkhd->rqhd", shares, block_value, preferred_element_type=jnp.float32
        ).astype(jnp.bfloat16)

    def by_block(tensor):
        return tensor.reshape((blocks, row_count // blocks) + tensor.shape[1:])

    result = lax.map(
        attend_one_block, (by_block(queries), by_block(key_part), by_block(value_part))
    )
    return result.reshape(row_count, query_feats, HEADS * HEAD_DIM)


def feature_layer(normed_cells, feat_out, key_part, value_part, queries):
    attended = attend_features(queries, key_part, value_part)
    update = jnp.dot(attended, feat_out, preferred_element_type=jnp.float32)
    return (normed_cells.astype(jnp.float32) + update).astype(jnp.bfloat16)


def on_device(cells, block_table, row_live, row_train, feat_qkv, feat_out, item_qkv, item_out):
    rows_here, feats_here, width_all = cells.shape
    row_index = lax.axis_index("rows")
    feat_index = lax.axis_index("feat")
    row_devices = lax.axis_size("rows")
    feat_devices = lax.axis_size("feat")
    my_table = lax.dynamic_index_in_dim(block_table, row_index, keepdims=False)
    live_rows = lax.dynamic_slice_in_dim(row_live, row_index * rows_here, rows_here).astype(
        jnp.float32
    )
    values = cells.astype(jnp.float32)
    table_hot = (jnp.arange(TABLES, dtype=jnp.int32) == my_table).astype(jnp.float32)
    first_local = jnp.sum(values * live_rows[:, None, None], axis=(0, 2))
    count_local = jnp.sum(live_rows) * width_all
    second_local = jnp.sum(values * values * live_rows[:, None, None], axis=(0, 2))
    first_sum, second_sum, count_sum = in_one(
        (
            table_hot[:, None] * first_local[None, :],
            table_hot[:, None] * second_local[None, :],
            table_hot * count_local,
        ),
        "rows",
    )
    table_mean = first_sum / count_sum[:, None]
    table_spread = second_sum / count_sum[:, None] - table_mean * table_mean
    mine_mean = lax.dynamic_index_in_dim(table_mean, my_table, keepdims=False)
    centred = values - mine_mean[None, :, None]
    mine_spread = lax.dynamic_index_in_dim(table_spread, my_table, keepdims=False)
    normed = (centred * lax.rsqrt(mine_spread + EPSILON)[None, :, None]).astype(jnp.bfloat16)
    normed_rows = lax.all_to_all(normed, "feat", split_axis=0, concat_axis=1, tiled=True)
    projected = jnp.dot(normed_rows, feat_qkv, preferred_element_type=jnp.float32).astype(
        jnp.bfloat16
    )
    queries = into_heads(projected[..., :width_all])
    key_part = into_heads(projected[..., width_all : 2 * width_all])
    value_part = into_heads(projected[..., 2 * width_all :])
    mixed_rows = feature_layer(normed_rows, feat_out, key_part, value_part, queries)
    group_rows, total_feats = (mixed_rows.shape[0], mixed_rows.shape[1])
    per_device = total_feats * HEADS // row_devices
    first_row = row_index * rows_here + feat_index * group_rows
    train_here = lax.dynamic_slice_in_dim(row_train, first_row, group_rows)
    places = compact_train(train_here)
    chosen = jnp.take(mixed_rows, places, axis=0)
    item_query = jnp.dot(
        mixed_rows, item_qkv[:, :width_all], preferred_element_type=jnp.float32
    ).astype(jnp.bfloat16)
    item_query = item_query.reshape(group_rows, row_devices, per_device, HEAD_DIM)
    key_value = jnp.dot(chosen, item_qkv[:, width_all:], preferred_element_type=jnp.float32).astype(
        jnp.bfloat16
    )
    item_key = key_value[..., :width_all].reshape(KEEP, row_devices, per_device, HEAD_DIM)
    item_value = key_value[..., width_all:].reshape(KEEP, row_devices, per_device, HEAD_DIM)
    query_table = jnp.repeat(block_table, group_rows)
    groups_all = row_train.reshape(row_devices, feat_devices, group_rows)
    group_counts = jnp.sum(groups_all, axis=2)
    slot_ids = jnp.arange(KEEP, dtype=jnp.int32)
    key_valid = slot_ids[None, None, :] < jnp.transpose(group_counts)[:, :, None]
    key_table = jnp.broadcast_to(block_table[None, :, None], key_valid.shape)
    allowed = (query_table[:, None] == key_table.reshape(-1)[None, :]) & key_valid.reshape(-1)[
        None, :
    ]
    query_count = query_table.shape[0]
    key_count = allowed.shape[1]
    query_blocks = max(1, query_count // 512)
    while query_count % query_blocks:
        query_blocks -= 1
    scaling = HEAD_DIM ** (-0.5)
    blocked_allowed = allowed.reshape(query_blocks, query_count // query_blocks, key_count)
    local_query = lax.all_to_all(item_query, "rows", split_axis=1, concat_axis=0, tiled=True)
    local_key = lax.all_to_all(item_key, "rows", split_axis=1, concat_axis=0, tiled=True)
    local_value = lax.all_to_all(item_value, "rows", split_axis=1, concat_axis=0, tiled=True)
    every_key, every_value = gather_together((local_key, local_value), "feat", (0, 0))

    def one_item(item_parts):
        single_query, single_key, single_value = item_parts

        def one_one_block(block_parts):
            block_query, block_allowed = block_parts
            scores = (
                jnp.dot(block_query, single_key.T, preferred_element_type=jnp.float32) * scaling
            )
            scores = jnp.where(block_allowed, scores, MASKED)
            shares = jax.nn.softmax(scores, axis=-1).astype(jnp.bfloat16)
            return jnp.dot(shares, single_value, preferred_element_type=jnp.float32).astype(
                jnp.bfloat16
            )

        blocked_query = single_query.reshape(query_blocks, query_count // query_blocks, HEAD_DIM)
        return lax.map(one_one_block, (blocked_query, blocked_allowed)).reshape(
            query_count, HEAD_DIM
        )

    by_item = (
        jnp.moveaxis(local_query[:, 0], 1, 0),
        jnp.moveaxis(every_key[:, 0], 1, 0),
        jnp.moveaxis(every_value[:, 0], 1, 0),
    )
    result = jnp.moveaxis(lax.map(one_item, by_item), 0, 1)[:, None]
    attended = lax.all_to_all(result, "rows", split_axis=0, concat_axis=1, tiled=True)
    attended = attended.reshape(group_rows, total_feats, width_all)
    update = jnp.dot(attended, item_out, preferred_element_type=jnp.float32)
    return (mixed_rows.astype(jnp.float32) + update).astype(jnp.bfloat16)


def solution(mesh):
    return jax.shard_map(
        on_device,
        mesh=mesh,
        in_specs=(P("rows", "feat", None), P(), P(), P(), P(), P(), P(), P()),
        out_specs=P(("rows", "feat"), None, None),
        check_vma=False,
    )
```

profile of v0, /device:TPU:1, one launch (start us, length us, event | category | flops | bytes accessed | tf_op | source)
XLA Modules:
  0.0 263.0 jit_solution(8148468147780909118)
XLA Ops:
  7.5 13.1 %all-to-all-start = ((f32[64,1,328]{2,1,0:T(1,128)}), f32[64,1,328]{2,1,0:T(1,128)S(1)}, u32[]{:S(2)}, u32[]{:S(2)}) async-start(f32[64,1,328]{2,1,0:T(1,128)} %broadcast_in_dim.81), calls=%async_computation | async-start | bytes 196608 | tf_op jit(solution)/shard_map/all_to_all | solution.py:18
  32.7 4.0 %all-to-all-start.1 = ((bf16[128,20,128]{2,1,0:T(8,128)(2,1)}), bf16[128,20,128]{2,1,0:T(8,128)(2,1)S(1)}, u32[]{:S(2)}, u32[]{:S(2)}) async-start(bf16[128,20,128]{2,1,0:T(8,128)(2,1)} %fusion.31), calls=%async_computation.1 | async-start | bytes 1572864 | tf_op jit(solution)/shard_map/all_to_all | solution.py:129
  36.8 11.7 %all-to-all-done.1 = bf16[128,20,128]{2,1,0:T(8,128)(2,1)S(1)} async-done(((bf16[128,20,128]{2,1,0:T(8,128)(2,1)}), bf16[128,20,128]{2,1,0:T(8,128)(2,1)S(1)}, u32[]{:S(2)}, u32[]{:S(2)}) %all-to-all-start.1) | async-done | bytes 655392 | tf_op jit(solution)/shard_map/all_to_all | solution.py:129
  52.2 10.6 %while.32 = (s32[]{:T(128)}, bf16[2,16,80,4,32]{2,4,3,1,0:T(8,128)(2,1)}, bf16[2,16,80,4,32]{2,4,3,1,0:T(8,128)(2,1)}, bf16[2,16,80,4,32]{2,4,3,1,0:T(8,128)(2,1...) while((s32[]{:T(128)}, bf16[2,16,80,4,32]{2,4,3,1,0:T(8,128)(2,1)}, ...), condition=%wide.region_7.8_spmd, body=%wide.region_4.7_spmd.sunk | while | flops 55050320 | bytes 12310625 | solution.py:88
  67.1 9.5 %all-to-all-start.3 = ((bf16[64,2,320]{2,1,0:T(2,128)(2,1)}), bf16[64,2,320]{2,1,0:T(2,128)(2,1)S(1)}, u32[]{:S(2)}, u32[]{:S(2)}) async-start(bf16[64,2,320]{2,1,0:T(2,128)(2,1)} %reshape.192), calls=%async_computation.3 | async-start | bytes 196608 | tf_op jit(solution)/shard_map/all_to_all | solution.py:169
  78.5 3.8 %reshape.164 = bf16[32,64,5,32]{3,2,1,0:T(8,128)(2,1)} reshape(bf16[32,80,128]{2,1,0:T(8,128)(2,1)S(1)} %convolution_convert_fusion.2) | data formatting | bytes 1310720 | tf_op jit(solution)/shard_map/reshape | solution.py:146
  82.4 5.2 %copy.144 = bf16[32,64,5,32]{3,0,2,1:T(8,128)(2,1)S(1)} copy(bf16[32,64,5,32]{3,2,1,0:T(8,128)(2,1)} %reshape.164) | data formatting | bytes 1310720 | tf_op jit(solution)/shard_map/reshape | solution.py:146
  90.2 10.3 %all-to-all-start.4 = ((bf16[64,2,320]{2,1,0:T(2,128)(2,1)}), bf16[64,2,320]{2,1,0:T(2,128)(2,1)S(1)}, u32[]{:S(2)}, u32[]{:S(2)}) async-start(bf16[64,2,320]{2,1,0:T(2,128)(2,1)} %reshape.190), calls=%async_computation.4 | async-start | bytes 196608 | tf_op jit(solution)/shard_map/all_to_all | solution.py:170
  101.3 9.4 %all-to-all-done.4 = bf16[64,2,320]{2,1,0:T(2,128)(2,1)S(1)} async-done(((bf16[64,2,320]{2,1,0:T(2,128)(2,1)}), bf16[64,2,320]{2,1,0:T(2,128)(2,1)S(1)}, u32[]{:S(2)}, u32[]{:S(2)}) %all-to-all-start.4) | async-done | bytes 81952 | tf_op jit(solution)/shard_map/all_to_all | solution.py:170
  110.7 4.5 %all-to-all-start.2 = ((bf16[64,2,2560]{2,1,0:T(2,128)(2,1)}), bf16[64,2,2560]{2,1,0:T(2,128)(2,1)S(1)}, u32[]{:S(2)}, u32[]{:S(2)}) async-start(bf16[64,2,2560]{2,1,0:T(2,128)(2,1)} %reshape.188), calls=%async_computation.2 | async-start | bytes 1310720 | tf_op jit(solution)/shard_map/all_to_all | solution.py:168
  116.0 11.3 %all-gather = bf16[327680]{0:T(1024)(128)(2,1)S(1)} all-gather(bf16[81920]{0:T(1024)(128)(2,1)S(1)} %pad_maximum_fusion), channel_id=2, replica_groups=mesh['rows'=64,'feat'=4] {'feat'}, dimensions={0}, use_global_device_ids=true | all-gather | bytes 819200 | tf_op jit(solution)/shard_map/all_gather | solution.py:45
  138.7 3.9 %copy.111 = bf16[64,32,1,5,32]{1,0,4,3,2:T(8,128)(2,1)S(1)} copy(bf16[64,32,1,5,32]{4,1,3,0,2:T(8,128)(2,1)} %bitcast_bitcast_fusion) | data formatting | bytes 1310720 | tf_op jit(solution)/shard_map/all_to_all | solution.py:168
  146.1 59.1 %while.34 = (s32[]{:T(128)}, bf16[5,2048,32]{2,1,0:T(8,128)(2,1)}, bf16[5,2048,32]{1,2,0:T(8,128)(2,1)}, bf16[5,1024,32]{2,1,0:T(8,128)(2,1)}, bf16[5,1024,32]{2...) while((s32[]{:T(128)}, bf16[5,2048,32]{2,1,0:T(8,128)(2,1)}, ...), condition=%wide.region_16.17_spmd.clone, body=%wide.region_11.16_spmd.clone.sunk | while | flops 75512832 | bytes 11330310 | solution.py:197
  149.9 6.9 %while.35 = (s32[]{:T(128)}, bf16[4,512,32]{1,2,0:T(8,128)(2,1)S(1)}, pred[4,512,1024]{2,1,0:T(32,128)(4,1)S(1)}, bf16[4,512,32]{2,1,0:T(8,128)(2,1)S(1)}, bf16[...) while((s32[]{:T(128)}, bf16[4,512,32]{1,2,0:T(8,128)(2,1)S(1)}, ...), condition=%wide.region_15.15_spmd, body=%wide.region_12.14_spmd.sunk | while | flops 71318528 | bytes 7515217 | solution.py:188
  161.7 6.9 %while.35 = (s32[]{:T(128)}, bf16[4,512,32]{1,2,0:T(8,128)(2,1)S(1)}, pred[4,512,1024]{2,1,0:T(32,128)(4,1)S(1)}, bf16[4,512,32]{2,1,0:T(8,128)(2,1)S(1)}, bf16[...) while((s32[]{:T(128)}, bf16[4,512,32]{1,2,0:T(8,128)(2,1)S(1)}, ...), condition=%wide.region_15.15_spmd, body=%wide.region_12.14_spmd.sunk | while | flops 71318528 | bytes 7515217 | solution.py:188
  173.5 6.9 %while.35 = (s32[]{:T(128)}, bf16[4,512,32]{1,2,0:T(8,128)(2,1)S(1)}, pred[4,512,1024]{2,1,0:T(32,128)(4,1)S(1)}, bf16[4,512,32]{2,1,0:T(8,128)(2,1)S(1)}, bf16[...) while((s32[]{:T(128)}, bf16[4,512,32]{1,2,0:T(8,128)(2,1)S(1)}, ...), condition=%wide.region_15.15_spmd, body=%wide.region_12.14_spmd.sunk | while | flops 71318528 | bytes 7515217 | solution.py:188
  185.4 6.9 %while.35 = (s32[]{:T(128)}, bf16[4,512,32]{1,2,0:T(8,128)(2,1)S(1)}, pred[4,512,1024]{2,1,0:T(32,128)(4,1)S(1)}, bf16[4,512,32]{2,1,0:T(8,128)(2,1)S(1)}, bf16[...) while((s32[]{:T(128)}, bf16[4,512,32]{1,2,0:T(8,128)(2,1)S(1)}, ...), condition=%wide.region_15.15_spmd, body=%wide.region_12.14_spmd.sunk | while | flops 71318528 | bytes 7515217 | solution.py:188
  197.2 6.9 %while.35 = (s32[]{:T(128)}, bf16[4,512,32]{1,2,0:T(8,128)(2,1)S(1)}, pred[4,512,1024]{2,1,0:T(32,128)(4,1)S(1)}, bf16[4,512,32]{2,1,0:T(8,128)(2,1)S(1)}, bf16[...) while((s32[]{:T(128)}, bf16[4,512,32]{1,2,0:T(8,128)(2,1)S(1)}, ...), condition=%wide.region_15.15_spmd, body=%wide.region_12.14_spmd.sunk | while | flops 71318528 | bytes 7515217 | solution.py:188
  205.2 5.1 %copy.143 = bf16[5,2048,32]{2,0,1:T(8,128)(2,1)} copy(bf16[5,2048,32]{2,1,0:T(8,128)(2,1)} %get-tuple-element.97) | data formatting | bytes 1310720 | tf_op jit(solution)/shard_map/while | solution.py:197
  210.3 5.4 %reshape.194 = bf16[64,2,2560]{2,1,0:T(2,128)(2,1)S(1)} reshape(bf16[2048,1,5,32]{3,2,1,0:T(8,128)(2,1)} %bitcast.147) | data formatting | bytes 1310720
  215.7 32.1 %all_to_all.84 = bf16[64,2,2560]{2,1,0:T(2,128)(2,1)S(1)} all-to-all(bf16[64,2,2560]{2,1,0:T(2,128)(2,1)S(1)} %reshape.194), channel_id=1, replica_groups=mesh['rows'=64,'feat'=4] {'rows'}, dimensions={0} | all-to-all | bytes 1310720 | tf_op jit(solution)/shard_map/all_to_all | solution.py:198
  247.8 4.0 %reshape.195 = bf16[2048,1,5,32]{3,2,1,0:T(8,128)(2,1)} reshape(bf16[64,2,2560]{2,1,0:T(2,128)(2,1)S(1)} %all_to_all.84) | data formatting | bytes 1310720
  251.8 5.3 %copy.142 = bf16[64,32,1,5,32]{4,3,0,1,2:T(8,128)(2,1)} copy(bf16[64,32,1,5,32]{4,3,1,0,2:T(8,128)(2,1)} %bitcast.148) | data formatting | bytes 1310720 | tf_op jit(solution)/shard_map/all_to_all | solution.py:198
  257.1 4.7 %reshape.171 = bf16[32,80,128]{2,1,0:T(8,128)(2,1)S(1)} reshape(bf16[32,64,1,5,32]{4,3,1,0,2:T(8,128)(2,1)} %bitcast.149) | data formatting | bytes 1310720 | tf_op jit(solution)/shard_map/reshape | solution.py:199
  (200 shorter events, 116.2 us)
Async XLA Ops:
  0.0 48.6 %copy-start = (bf16[128,384]{1,0:T(8,128)(2,1)S(1)}, bf16[128,384]{1,0:T(8,128)(2,1)}, u32[]{:S(2)}) copy-start(bf16[128,384]{1,0:T(8,128)(2,1)} %param.18) | copy-start | bytes 294916
  0.0 31.4 %copy-start.4 = (bf16[128,20,128]{2,0,1:T(8,128)(2,1)S(1)}, bf16[128,20,128]{2,0,1:T(8,128)(2,1)}, u32[]{:S(2)}) copy-start(bf16[128,20,128]{2,0,1:T(8,128)(2,1)} %param.14) | copy-start | bytes 1966084
  7.5 23.3 %all-to-all-start = ((f32[64,1,328]{2,1,0:T(1,128)}), f32[64,1,328]{2,1,0:T(1,128)S(1)}, u32[]{:S(2)}, u32[]{:S(2)}) async-start(f32[64,1,328]{2,1,0:T(1,128)} %broadcast_in_dim.81), calls=%async_computation | async-start | bytes 196608 | tf_op jit(solution)/shard_map/all_to_all | solution.py:18
  32.7 15.7 %all-to-all-start.1 = ((bf16[128,20,128]{2,1,0:T(8,128)(2,1)}), bf16[128,20,128]{2,1,0:T(8,128)(2,1)S(1)}, u32[]{:S(2)}, u32[]{:S(2)}) async-start(bf16[128,20,128]{2,1,0:T(8,128)(2,1)} %fusion.31), calls=%async_computation.1 | async-start | bytes 1572864 | tf_op jit(solution)/shard_map/all_to_all | solution.py:129
  52.2 10.6 %copy-start.7 = (bf16[128,128]{1,0:T(8,128)(2,1)S(1)}, bf16[128,128]{1,0:T(8,128)(2,1)}, u32[]{:S(2)}) copy-start(bf16[128,128]{1,0:T(8,128)(2,1)} %param.19) | copy-start | bytes 98308
  52.8 3.4 %copy-start.5 = (bf16[2,16,80,4,32]{2,4,3,1,0:T(8,128)(2,1)S(1)}, bf16[2,16,80,4,32]{2,4,3,1,0:T(8,128)(2,1)}, u32[]{:S(2)}) copy-start(bf16[2,16,80,4,32]{2,4,3,1,0:T(8,128)(2,1)} %get-tuple-element.407) | copy-start | bytes 1966084 | tf_op jit(solution)/shard_map/while
  58.1 3.4 %copy-start.5 = (bf16[2,16,80,4,32]{2,4,3,1,0:T(8,128)(2,1)S(1)}, bf16[2,16,80,4,32]{2,4,3,1,0:T(8,128)(2,1)}, u32[]{:S(2)}) copy-start(bf16[2,16,80,4,32]{2,4,3,1,0:T(8,128)(2,1)} %get-tuple-element.407) | copy-start | bytes 1966084 | tf_op jit(solution)/shard_map/while
  62.8 2.3 copy-start.6
  64.6 13.6 %copy-start.2 = (bf16[32,80,128]{2,1,0:T(8,128)(2,1)}, bf16[32,80,128]{2,1,0:T(8,128)(2,1)S(1)}, u32[]{:S(2)}) copy-start(bf16[32,80,128]{2,1,0:T(8,128)(2,1)S(1)} %fusion.32) | copy-start | bytes 1966084
  67.1 23.1 %all-to-all-start.3 = ((bf16[64,2,320]{2,1,0:T(2,128)(2,1)}), bf16[64,2,320]{2,1,0:T(2,128)(2,1)S(1)}, u32[]{:S(2)}, u32[]{:S(2)}) async-start(bf16[64,2,320]{2,1,0:T(2,128)(2,1)} %reshape.192), calls=%async_computation.3 | async-start | bytes 196608 | tf_op jit(solution)/shard_map/all_to_all | solution.py:169
  90.2 20.5 %all-to-all-start.4 = ((bf16[64,2,320]{2,1,0:T(2,128)(2,1)}), bf16[64,2,320]{2,1,0:T(2,128)(2,1)S(1)}, u32[]{:S(2)}, u32[]{:S(2)}) async-start(bf16[64,2,320]{2,1,0:T(2,128)(2,1)} %reshape.190), calls=%async_computation.4 | async-start | bytes 196608 | tf_op jit(solution)/shard_map/all_to_all | solution.py:170
  110.7 24.6 %all-to-all-start.2 = ((bf16[64,2,2560]{2,1,0:T(2,128)(2,1)}), bf16[64,2,2560]{2,1,0:T(2,128)(2,1)S(1)}, u32[]{:S(2)}, u32[]{:S(2)}) async-start(bf16[64,2,2560]{2,1,0:T(2,128)(2,1)} %reshape.188), calls=%async_computation.2 | async-start | bytes 1310720 | tf_op jit(solution)/shard_map/all_to_all | solution.py:168
  257.1 4.7 %copy-start.3 = (bf16[32,80,128]{2,1,0:T(8,128)(2,1)S(1)}, bf16[32,80,128]{2,1,0:T(8,128)(2,1)}, u32[]{:S(2)}) copy-start(bf16[32,80,128]{2,1,0:T(8,128)(2,1)} %copy-done.2) | copy-start | bytes 1966084
  257.1 4.7 %copy-start.8 = (bf16[128,128]{1,0:T(8,128)(2,1)S(1)}, bf16[128,128]{1,0:T(8,128)(2,1)}, u32[]{:S(2)}) copy-start(bf16[128,128]{1,0:T(8,128)(2,1)} %param.21) | copy-start | bytes 98308
  257.1 5.9 %copy-start.1 = (bf16[128,384]{1,0:T(8,128)(2,1)S(1)}, bf16[128,384]{1,0:T(8,128)(2,1)}, u32[]{:S(2)}) copy-start(bf16[128,384]{1,0:T(8,128)(2,1)} %param.18) | copy-start | bytes 294916
where the time goes:
time: 264 us; the launch traced here: 263 us
  local copies, waits for them, and re-layouts  85.9 us (33%)
  blocking collectives  43.3 us (16%)
  starting transfers between devices  41.4 us (16%)
  other arithmetic  33.3 us (13%)
  matrix products  31.7 us (12%)
  waiting for transfers between devices  23.7 us (9%)
  between operations  3.17 us (1%)
    all_to_all x1, blocking collectives, on_device(): lax.all_to_all(result, 'rows', split_axis=0, concat_axis=1, tiled=True)  32.1 us
    unnamed x26, local copies, waits for them, and re-layouts  18.4 us
    all_to_all x1, starting transfers between devices, from_everyone(): lax.all_to_all(jnp.broadcast_to(shard[None], (peers, *shard.shape)), axis...  13.1 us
    dot_general x20, matrix products, one_one_block(): jnp.dot(block_query, single_key.T, preferred_element_type=jnp.float32)  12 us
    dot_general x20, matrix products, one_one_block(): jnp.dot(shares, single_value, preferred_element_type=jnp.float32)  12 us
    all_to_all x1, waiting for transfers between devices, on_device(): lax.all_to_all(normed, 'feat', split_axis=0, concat_axis=1, tiled=True)  11.7 us
    all_gather x1, blocking collectives, gather_together(): lines, at, done = (lax.all_gather(vector, axis), 0, [])  11.3 us
    reduce_sum x20, other arithmetic, one_one_block(): shares = jax.nn.softmax(scores, axis=-1).astype(jnp.bfloat16)  10.3 us
  transfers between devices with their start and end apart: 5, of which 4 were waited for; matrix products, arithmetic and copies ran while one was open for 11% of the time, Pallas kernels for 0%

commit v1 on v0

v1 whole, which is shorter than its diff:
```python
import jax
import jax.numpy as jnp
from jax import lax
from jax.experimental import pallas as pl
from jax.experimental.pallas import tpu as pltpu
from jax.sharding import PartitionSpec as P

HEADS = 4
HEAD_DIM = 32
WIDTH = 128
KEEP = 4
XS, YS, ZS, CS = 4, 4, 8, 2
BLOCKS = YS * ZS * CS
BLOCK = 128
FEATS = 80
SHARD = 20
OWNED = 5
GROUP = 32
OWNERS = XS * YS
PLACES = ZS * CS
KEYS = YS * XS * KEEP
TILE = 256
EPSILON = 1e-05
MASKED = -1e30
SCALE = HEAD_DIM**-0.5 * 1.4426950408889634
MESH = pl.DeviceIdType.MESH
F32 = jnp.float32
BF16 = jnp.bfloat16
VMEM = pl.BlockSpec(memory_space=pltpu.VMEM)
SMEM = pl.BlockSpec(memory_space=pltpu.SMEM)
ANY = pl.BlockSpec(memory_space=pl.ANY)


def iota(shape, dim):
    return lax.broadcasted_iota(jnp.int32, shape, dim)


def row_of(y, z, c):
    return y * (ZS * CS) + z * CS + c


def around(at, step, size):
    return lax.rem(at + step + size, size)


def remote(source, target, send, recv, row, feat):
    return pltpu.make_async_remote_copy(
        src_ref=source,
        dst_ref=target,
        send_sem=send,
        recv_sem=recv,
        device_id=(row, feat),
        device_id_type=MESH,
    )


def position():
    row = lax.axis_index("rows")
    x = lax.axis_index("feat")
    y = lax.div(row, ZS * CS)
    z = lax.rem(lax.div(row, CS), ZS)
    c = lax.rem(row, CS)
    return row, x, y, z, c


def mix_kernel(
    cells, table, live, train, wqkv, wout, q_out, kv_out,
    own, xbuf, st_src, sx, sy_src, sy, sz, nrm, qkv, att, mix, send,
    own_sem, xs, xr, ss, sr, ys, yr, zs, zr, qs, qr, rs, rr, ls, lr, ps, pr,
):
    row, x, y, z, c = position()
    owner = y * XS + x

    fetch = pltpu.make_async_copy(cells, own, own_sem.at[0])
    fetch.start()
    barrier = pltpu.get_barrier_semaphore()
    greet = []
    for dy in range(YS):
        for dx in range(XS):
            if dx or dy:
                greet.append((row_of(around(y, dy, YS), z, c), around(x, dx, XS)))
        greet.append((row_of(around(y, dy, YS), z, 1 - c), x))
    for dz in range(1, ZS):
        greet.append((row_of(y, around(z, dz, ZS), c), x))
    for peer in greet:
        pl.semaphore_signal(barrier, inc=1, device_id=peer, device_id_type=MESH)
    fetch.wait()

    base = row * BLOCK

    def add_first(r, carry):
        total, count = carry
        w = live[base + r]
        return total + w.astype(F32) * own[r].astype(F32), count + w

    total, count = lax.fori_loop(
        0, BLOCK, add_first, (jnp.zeros((SHARD, WIDTH), F32), jnp.int32(0)), unroll=8
    )
    first = jnp.sum(total, axis=1, keepdims=True)
    entries = jnp.full((SHARD, WIDTH), count.astype(F32) * WIDTH, F32)
    mean_here = jnp.broadcast_to(first, (SHARD, WIDTH)) / entries

    def add_second(r, total):
        off = own[r].astype(F32) - mean_here
        return total + live[base + r].astype(F32) * (off * off)

    second = jnp.sum(
        lax.fori_loop(0, BLOCK, add_second, jnp.zeros((SHARD, WIDTH), F32), unroll=8),
        axis=1,
        keepdims=True,
    )
    lane = iota((SHARD, WIDTH), 1)
    sub = iota((SHARD, WIDTH), 0)
    spot = lane == sub + GROUP * x

    def to_row(column):
        return jnp.sum(jnp.where(spot, column, 0.0), axis=0, keepdims=True)

    st_src[...] = jnp.concatenate(
        [to_row(first), to_row(second), to_row(entries), jnp.zeros((5, WIDTH), F32)], axis=0
    )
    pl.semaphore_wait(barrier, len(greet))

    stat_x = []
    for d in range(1, XS):
        copy = remote(st_src, sx.at[x], ss.at[d], sr.at[d], row, around(x, d, XS))
        copy.start()
        stat_x.append(copy)
    bulk = []
    for d in (1, 3, 2):
        to = around(x, d, XS)
        copy = remote(
            cells.at[pl.ds(to * GROUP, GROUP)], xbuf.at[x], xs.at[d], xr.at[d], row, to
        )
        copy.start()
        bulk.append((d, copy))
    keep = pltpu.make_async_copy(own.at[pl.ds(x * GROUP, GROUP)], xbuf.at[x], own_sem.at[1])
    keep.start()
    sx[x] = st_src[...]
    for d in range(1, XS):
        came = around(x, -d, XS)
        remote(st_src, sx.at[came], ss.at[d], sr.at[d], row, x).wait_recv()
    merged = sx[0] + sx[1] + sx[2] + sx[3]
    sy_src[...] = merged
    here = y * CS + c
    sy[here] = merged
    stat_y = []
    for dy in range(YS):
        for dc in range(CS):
            if dy or dc:
                k = dy * CS + dc
                to = row_of(around(y, dy, YS), z, around(c, dc, CS))
                copy = remote(sy_src, sy.at[here], ys.at[k], yr.at[k], to, x)
                copy.start()
                stat_y.append(copy)
    for dy in range(YS):
        for dc in range(CS):
            if dy or dc:
                k = dy * CS + dc
                came = around(y, -dy, YS) * CS + around(c, dc, CS)
                remote(sy_src, sy.at[came], ys.at[k], yr.at[k], row, x).wait_recv()
    stat_z = []
    for d in range(1, ZS):
        copy = remote(
            sy, sz.at[z], zs.at[d], zr.at[d], row_of(y, around(z, d, ZS), c), x
        )
        copy.start()
        stat_z.append(copy)
    sz[z] = sy[...]
    for d in range(1, ZS):
        came = around(z, -d, ZS)
        remote(sy, sz.at[came], zs.at[d], zr.at[d], row, x).wait_recv()

    mine = table[row]
    weights = []
    acc = jnp.zeros((8, WIDTH), F32)
    for zz in range(ZS):
        for yc in range(YS * CS):
            at = row_of(yc // CS, zz, yc % CS)
            w = jnp.where(table[at] == mine, 1.0, 0.0).astype(F32)
            weights.append(w)
            acc = acc + w * sz[zz, yc]
    entries_all = acc[2:3]
    mean_row = acc[0:1] / entries_all
    spread = jnp.zeros((1, WIDTH), F32)
    for zz in range(ZS):
        for yc in range(YS * CS):
            tile = sz[zz, yc]
            off = tile[0:1] / tile[2:3] - mean_row
            spread = spread + weights[zz * YS * CS + yc] * (tile[1:2] + tile[2:3] * (off * off))
    inv_row = lax.rsqrt(spread / entries_all + EPSILON)

    for _, copy in bulk:
        copy.wait_recv()
    keep.wait()
    for s in range(XS):
        pick = lane == sub + GROUP * s
        mean_col = jnp.broadcast_to(
            jnp.sum(jnp.where(pick, mean_row, 0.0), axis=1, keepdims=True), (SHARD, WIDTH)
        )
        inv_col = jnp.broadcast_to(
            jnp.sum(jnp.where(pick, inv_row, 0.0), axis=1, keepdims=True), (SHARD, WIDTH)
        )

        def norm(r, none, s=s, mean_col=mean_col, inv_col=inv_col):
            value = (xbuf[s, r].astype(F32) - mean_col) * inv_col
            nrm[r, SHARD * s : SHARD * (s + 1), :] = value.astype(BF16).astype(F32)
            return none

        lax.fori_loop(0, GROUP, norm, 0, unroll=4)

    def project(i, none):
        part = nrm[pl.ds(i * 4, 4)].reshape(4 * FEATS, WIDTH).astype(BF16)
        out = jnp.dot(part, wqkv[...], preferred_element_type=F32)
        qkv[pl.ds(i * 4, 4), :, 0:WIDTH] = (
            (out[:, :WIDTH] * SCALE).astype(BF16).reshape(4, FEATS, WIDTH)
        )
        qkv[pl.ds(i * 4, 4), :, WIDTH:] = (
            out[:, WIDTH:].astype(BF16).reshape(4, FEATS, 2 * WIDTH)
        )
        return none

    lax.fori_loop(0, GROUP // 4, project, 0)

    head = iota((FEATS, WIDTH), 1) // HEAD_DIM
    ones = jnp.ones((FEATS, WIDTH), BF16)

    def attend(r, none):
        query = qkv[r, :, 0:WIDTH]
        key = qkv[r, :, WIDTH : 2 * WIDTH]
        value = jnp.concatenate([qkv[r, :, 2 * WIDTH :], ones], axis=1)
        stacked = jnp.concatenate(
            [jnp.where(head == h, query, jnp.zeros_like(query)) for h in range(HEADS)], axis=0
        )
        scores = lax.dot_general(
            stacked, key, (((1,), (1,)), ((), ())), preferred_element_type=F32
        )
        top = jnp.max(scores, axis=1, keepdims=True)
        shares = jnp.exp2(scores - top).astype(BF16)
        out = jnp.dot(shares, value, preferred_element_type=F32)
        num = out[0:FEATS, :WIDTH]
        den = out[0:FEATS, WIDTH:]
        for h in range(1, HEADS):
            num = jnp.where(head == h, out[h * FEATS : (h + 1) * FEATS, :WIDTH], num)
            den = jnp.where(head == h, out[h * FEATS : (h + 1) * FEATS, WIDTH:], den)
        att[r] = (num / den).astype(BF16)
        return none

    lax.fori_loop(0, GROUP, attend, 0)

    def update(i, none):
        part = att[pl.ds(i * 4, 4)].reshape(4 * FEATS, WIDTH)
        out = jnp.dot(part, wout[...], preferred_element_type=F32)
        out = out + nrm[pl.ds(i * 4, 4)].reshape(4 * FEATS, WIDTH)
        mix[pl.ds(i * 4 * FEATS, 4 * FEATS), :] = out
        return none

    lax.fori_loop(0, GROUP // 4, update, 0)

    def turn(f, none):
        send[f] = mix[pl.ds(f, GROUP, stride=FEATS), :].astype(BF16)
        return none

    lax.fori_loop(0, FEATS, turn, 0, unroll=4)

    moved = []
    for dy in range(YS):
        for dx in range(XS):
            if dx or dy:
                k = dy * XS + dx
                ty, tx = around(y, dy, YS), around(x, dx, XS)
                copy = remote(
                    send.at[pl.ds((ty * XS + tx) * OWNED, OWNED)],
                    q_out.at[owner],
                    qs.at[k],
                    qr.at[k],
                    row_of(ty, z, c),
                    tx,
                )
                copy.start()
                moved.append(copy)
    q_out[owner] = send[pl.ds(owner * OWNED, OWNED)]
    lane = iota((BLOCK, BLOCK), 1)
    sub = iota((BLOCK, BLOCK), 0)
    lower = ((sub // GROUP == lane // GROUP) & (sub <= lane)).astype(F32).astype(BF16)
    place = iota((OWNERS, BLOCK), 0)
    along = iota((OWNERS, BLOCK), 1)
    picks = []
    for yy in range(YS):
        flags = jnp.broadcast_to(
            train[pl.ds(row_of(yy, z, c), 1), :].astype(F32), (OWNERS, BLOCK)
        )
        ordinal = jnp.dot(flags.astype(BF16), lower, preferred_element_type=F32)
        wanted = (place % KEEP + 1).astype(F32)
        hit = (flags > 0.5) & (ordinal == wanted) & (along // GROUP == place // KEEP)
        picks.append(hit.astype(F32).astype(BF16))
    for copy in moved:
        copy.wait_recv()

    spot_here = z * CS + c
    for yy in range(YS):
        for f in range(OWNED):
            rows = jnp.concatenate([q_out[yy * XS + xx, f] for xx in range(XS)], axis=0)
            kv_out[spot_here, f, yy * 16 : yy * 16 + 16, :] = jnp.dot(
                picks[yy], rows, preferred_element_type=F32
            ).astype(BF16)

    right, left = row_of(y, around(z, 1, ZS), c), row_of(y, around(z, -1, ZS), c)
    other = row_of(y, z, 1 - c)

    def slot(d):
        return around(z, d, ZS) * CS + c

    def over(d):
        k = d + 4
        copy = remote(kv_out.at[slot(d)], kv_out.at[slot(d)], ps.at[k], pr.at[k], other, x)
        copy.start()
        sent.append(copy)

    sent = []
    for k in range(4):
        copy = remote(kv_out.at[slot(-k)], kv_out.at[slot(-k)], rs.at[k], rr.at[k], right, x)
        copy.start()
        sent.append(copy)
        if k < 3:
            copy = remote(kv_out.at[slot(k)], kv_out.at[slot(k)], ls.at[k], lr.at[k], left, x)
            copy.start()
            sent.append(copy)
        if k == 0:
            over(0)
        came = kv_out.at[slot(-1 - k)]
        remote(came, came, rs.at[k], rr.at[k], right, x).wait_recv()
        over(-1 - k)
        if k < 3:
            came = kv_out.at[slot(1 + k)]
            remote(came, came, ls.at[k], lr.at[k], left, x).wait_recv()
            over(1 + k)
    for d in range(-4, 4):
        came = kv_out.at[around(z, d, ZS) * CS + 1 - c]
        remote(came, came, ps.at[d + 4], pr.at[d + 4], other, x).wait_recv()

    for copy in stat_x + [copy for _, copy in bulk] + stat_y + stat_z + moved + sent:
        copy.wait_send()


def item_kernel(q_in, kv_in, table, train, wqkv, wout, out, qp, kvp, kvc, bias):
    row, x, y, z, c = position()
    kvc[...] = jnp.zeros_like(kvc)

    def project_q(i, none):
        part = q_in[i].reshape(OWNED * GROUP, WIDTH)
        got = jnp.dot(part, wqkv[:, :WIDTH], preferred_element_type=F32)
        qp[i] = (got * SCALE).astype(BF16).reshape(OWNED, GROUP, WIDTH)
        return none

    lax.fori_loop(0, OWNERS, project_q, 0)

    def project_kv(i, none):
        part = kv_in[i].reshape(OWNED * KEYS, WIDTH)
        got = jnp.dot(part, wqkv[:, WIDTH:], preferred_element_type=F32)
        kvp[i] = got.astype(BF16).reshape(OWNED, KEYS, 2 * WIDTH)
        return none

    lax.fori_loop(0, PLACES, project_kv, 0)

    group = (iota((OWNERS, BLOCK), 1) // GROUP == iota((OWNERS, BLOCK), 0) // KEEP)
    counts = lax.dot_general(
        group.astype(F32).astype(BF16),
        train[...].astype(F32).astype(BF16),
        (((1,), (1,)), ((), ())),
        preferred_element_type=F32,
    )
    number = (iota((OWNERS, BLOCKS), 0) % KEEP).astype(F32)
    bias_all = jnp.where(number < counts, 0.0, MASKED)
    which = iota((OWNERS, BLOCKS), 1)
    head = iota((BLOCK, WIDTH), 1) // HEAD_DIM

    def one_block(yy, none):
        mine = table[row_of(yy, z, c)]

        def gather(j, n):
            hit = table[j] == mine

            @pl.when(hit)
            def _():
                at = pl.multiple_of(n * 16, 16)
                come = pl.multiple_of(lax.div(j, PLACES) * 16, 16)
                for f in range(OWNED):
                    kvc[f, pl.ds(at, 16), :] = kvp[lax.rem(j, PLACES), f, pl.ds(come, 16), :]
                column = jnp.sum(jnp.where(which == j, bias_all, 0.0), axis=1, keepdims=True)
                bias[pl.ds(at, 16), :] = jnp.broadcast_to(column, (16, WIDTH))

            return n + hit.astype(jnp.int32)

        n = lax.fori_loop(0, BLOCKS, gather, jnp.int32(0))
        tiles = lax.div(n + 15, 16)

        def tail(i, none):
            bias[pl.ds(pl.multiple_of(i * 16, 16), 16), :] = jnp.full((16, WIDTH), MASKED, F32)
            return none

        lax.fori_loop(n, tiles * 16, tail, 0)

        def one_feature(f, none):
            query = jnp.concatenate([qp[yy * XS + xx, f] for xx in range(XS)], axis=0)
            stacked = jnp.concatenate(
                [jnp.where(head == h, query, jnp.zeros_like(query)) for h in range(HEADS)],
                axis=0,
            )

            def one_tile(kt, carry):
                top, total, acc = carry
                at = pl.multiple_of(kt * TILE, TILE)
                key = kvc[f, pl.ds(at, TILE), 0:WIDTH]
                value = kvc[f, pl.ds(at, TILE), WIDTH:]
                scores = lax.dot_general(
                    key, stacked, (((1,), (1,)), ((), ())), preferred_element_type=F32
                )
                mask = bias[pl.ds(at, TILE), :]
                scores = scores + jnp.concatenate([mask] * HEADS, axis=1)
                new_top = jnp.maximum(top, jnp.max(scores, axis=0, keepdims=True))
                shares = jnp.exp2(scores - new_top)
                fade = jnp.exp2(top - new_top)
                total = total * fade + jnp.sum(shares, axis=0, keepdims=True)
                got = lax.dot_general(
                    value, shares.astype(BF16), (((0,), (0,)), ((), ())),
                    preferred_element_type=F32,
                )
                parts = []
                for h in range(HEADS):
                    rows = slice(h * HEAD_DIM, (h + 1) * HEAD_DIM)
                    cols = slice(h * BLOCK, (h + 1) * BLOCK)
                    parts.append(acc[rows] * fade[:, cols] + got[rows, cols])
                return new_top, total, jnp.concatenate(parts, axis=0)

            top, total, acc = lax.fori_loop(
                0,
                tiles,
                one_tile,
                (
                    jnp.full((1, HEADS * BLOCK), MASKED, F32),
                    jnp.zeros((1, HEADS * BLOCK), F32),
                    jnp.zeros((WIDTH, BLOCK), F32),
                ),
            )
            attended = jnp.concatenate(
                [
                    acc[h * HEAD_DIM : (h + 1) * HEAD_DIM] / total[:, h * BLOCK : (h + 1) * BLOCK]
                    for h in range(HEADS)
                ],
                axis=0,
            ).astype(BF16)
            got = lax.dot_general(
                attended, wout[...], (((0,), (0,)), ((), ())), preferred_element_type=F32
            )
            for xx in range(XS):
                mixed = q_in[yy * XS + xx, f].astype(F32)
                out[yy * XS + xx, f] = (mixed + got[xx * GROUP : (xx + 1) * GROUP]).astype(BF16)
            return none

        lax.fori_loop(0, OWNED, one_feature, 0)
        return none

    lax.fori_loop(0, YS, one_block, 0)


def back_kernel(done, out, send_sems, recv_sems):
    row, x, y, z, c = position()
    owner = y * XS + x
    barrier = pltpu.get_barrier_semaphore()
    for dy in range(YS):
        for dx in range(XS):
            if dx or dy:
                peer = (row_of(around(y, dy, YS), z, c), around(x, dx, XS))
                pl.semaphore_signal(barrier, inc=1, device_id=peer, device_id_type=MESH)
    pl.semaphore_wait(barrier, OWNERS - 1)
    sent = []
    for dy in range(YS):
        for dx in range(XS):
            if dx or dy:
                k = dy * XS + dx
                ty, tx = around(y, dy, YS), around(x, dx, XS)
                copy = remote(
                    done.at[ty * XS + tx],
                    out.at[owner],
                    send_sems.at[k],
                    recv_sems.at[k],
                    row_of(ty, z, c),
                    tx,
                )
                copy.start()
                sent.append(copy)
    out[owner] = done[owner]
    for copy in sent:
        copy.wait_recv()
    for copy in sent:
        copy.wait_send()


def turn_kernel(rows, out, wide):
    def widen(g, none):
        wide[pl.ds(pl.multiple_of(g * OWNED * GROUP, 32), OWNED * GROUP), :] = (
            rows[g].reshape(OWNED * GROUP, WIDTH).astype(F32)
        )
        return none

    lax.fori_loop(0, OWNERS, widen, 0)

    def turn(r, none):
        out[r] = wide[pl.ds(r, FEATS, stride=GROUP), :].astype(BF16)
        return none

    lax.fori_loop(0, GROUP, turn, 0, unroll=4)


def on_device(cells, block_table, row_live, row_train, feat_qkv, feat_out, item_qkv, item_out):
    train = row_train.reshape(BLOCKS, BLOCK)
    dma = pltpu.SemaphoreType.DMA
    moved = jax.ShapeDtypeStruct((OWNERS, OWNED, GROUP, WIDTH), BF16)
    query, key = pl.pallas_call(
        mix_kernel,
        name="mix",
        out_shape=(moved, jax.ShapeDtypeStruct((PLACES, OWNED, KEYS, WIDTH), BF16)),
        in_specs=[ANY, SMEM, SMEM, VMEM, VMEM, VMEM],
        out_specs=(VMEM, VMEM),
        scratch_shapes=[
            pltpu.VMEM((BLOCK, SHARD, WIDTH), BF16),
            pltpu.VMEM((XS, GROUP, SHARD, WIDTH), BF16),
            pltpu.VMEM((8, WIDTH), F32),
            pltpu.VMEM((XS, 8, WIDTH), F32),
            pltpu.VMEM((8, WIDTH), F32),
            pltpu.VMEM((YS * CS, 8, WIDTH), F32),
            pltpu.VMEM((ZS, YS * CS, 8, WIDTH), F32),
            pltpu.VMEM((GROUP, FEATS, WIDTH), F32),
            pltpu.VMEM((GROUP, FEATS, 3 * WIDTH), BF16),
            pltpu.VMEM((GROUP, FEATS, WIDTH), BF16),
            pltpu.VMEM((GROUP * FEATS, WIDTH), F32),
            pltpu.VMEM((FEATS, GROUP, WIDTH), BF16),
            dma((2,)),
            dma((XS,)), dma((XS,)), dma((XS,)), dma((XS,)),
            dma((8,)), dma((8,)), dma((8,)), dma((8,)),
            dma((OWNERS,)), dma((OWNERS,)),
            dma((4,)), dma((4,)), dma((4,)), dma((4,)), dma((8,)), dma((8,)),
        ],
        compiler_params=pltpu.CompilerParams(collective_id=0, has_side_effects=True),
    )(cells, block_table, row_live, train, feat_qkv, feat_out)
    done = pl.pallas_call(
        item_kernel,
        name="item",
        out_shape=moved,
        in_specs=[VMEM, VMEM, SMEM, VMEM, VMEM, VMEM],
        out_specs=VMEM,
        scratch_shapes=[
            pltpu.VMEM((OWNERS, OWNED, GROUP, WIDTH), BF16),
            pltpu.VMEM((PLACES, OWNED, KEYS, 2 * WIDTH), BF16),
            pltpu.VMEM((OWNED, PLACES * KEYS, 2 * WIDTH), BF16),
            pltpu.VMEM((PLACES * KEYS, WIDTH), F32),
        ],
    )(query, key, block_table, train, item_qkv, item_out)
    rows = pl.pallas_call(
        back_kernel,
        name="back",
        out_shape=moved,
        in_specs=[VMEM],
        out_specs=VMEM,
        scratch_shapes=[dma((OWNERS,)), dma((OWNERS,))],
        compiler_params=pltpu.CompilerParams(collective_id=1, has_side_effects=True),
    )(done)
    return pl.pallas_call(
        turn_kernel,
        name="turn",
        out_shape=jax.ShapeDtypeStruct((GROUP, FEATS, WIDTH), BF16),
        in_specs=[VMEM],
        out_specs=VMEM,
        scratch_shapes=[pltpu.VMEM((FEATS * GROUP, WIDTH), F32)],
    )(rows)


def solution(mesh):
    return jax.shard_map(
        on_device,
        mesh=mesh,
        in_specs=(P("rows", "feat", None), P(), P(), P(), P(), P(), P(), P()),
        out_specs=P(("rows", "feat"), None, None),
        check_vma=False,
    )
```

time: 264 us -> 128 us (0.48)
  Pallas kernels: 0 us -> 127 us
  local copies, waits for them, and re-layouts: 85.9 us -> 2.46 us
  blocking collectives: 43.3 us -> 0 us
  starting transfers between devices: 41.4 us -> 0 us
  other arithmetic: 33.3 us -> 0 us
  matrix products: 31.7 us -> 0 us
  waiting for transfers between devices: 23.7 us -> 0 us
  between operations: 3.17 us -> 0.02 us
    pallas_call x0 -> x4, Pallas kernels: none -> 127 us  [the longest x1 76.2 us: on_device(): pl.pallas_call(mix_kernel, name='mix', out_shape=(moved, jax.ShapeDtypeSt...]
    all_to_all x5 -> x0, starting transfers between devices: 41.4 us -> none  [the longest x1 13.1 us: from_everyone(): lax.all_to_all(jnp.broadcast_to(shard[None], (peers, *shard.shape)), axis...]
    all_to_all x1 -> x0, blocking collectives: 32.1 us -> none  [on_device(): lax.all_to_all(result, 'rows', split_axis=0, concat_axis=1, tiled=True)]
    dot_general x49 -> x0, matrix products: 31.7 us -> none  [the longest x20 12 us: one_one_block(): jnp.dot(block_query, single_key.T, preferred_element_type=jnp.float32)]
    all_to_all x5 -> x0, waiting for transfers between devices: 23.7 us -> none  [the longest x1 11.7 us: on_device(): lax.all_to_all(normed, 'feat', split_axis=0, concat_axis=1, tiled=True)]
    reshape x12 -> x0, local copies, waits for them, and re-layouts: 16.7 us -> none  [the longest x2 9.04 us: on_device(): item_query.reshape(group_rows, row_devices, per_device, HEAD_DIM)]
    unnamed x26 -> x1, local copies, waits for them, and re-layouts: 18.4 us -> 2.46 us
    reduce_sum x25 -> x0, other arithmetic: 14.8 us -> none  [the longest x20 10.3 us: one_one_block(): shares = jax.nn.softmax(scores, axis=-1).astype(jnp.bfloat16)]
  transfers between devices with their start and end apart: 5 -> 0, of which waited for: 4 -> 0; matrix products, arithmetic and copies ran while one was open for 11% -> 0% of each run, Pallas kernels for 0% -> 0%
where the time goes in v1:
time: 128 us; the launch traced here: 129 us
  Pallas kernels  127 us (99%)
  local copies, waits for them, and re-layouts  2.46 us (2%)
    pallas_call x1, Pallas kernels, on_device(): pl.pallas_call(mix_kernel, name='mix', out_shape=(moved, jax.ShapeDtypeSt...  76.2 us
    pallas_call x1, Pallas kernels, on_device(): pl.pallas_call(item_kernel, name='item', out_shape=moved, in_specs=[VMEM,...  35.2 us
    pallas_call x1, Pallas kernels, on_device(): pl.pallas_call(back_kernel, name='back', out_shape=moved, in_specs=[VMEM]...  12.4 us
    pallas_call x1, Pallas kernels, on_device(): pl.pallas_call(turn_kernel, name='turn', out_shape=jax.ShapeDtypeStruct((...  3.03 us

profile of v1, /device:TPU:1, one launch (start us, length us, event | category | flops | bytes accessed | tf_op | source)
XLA Modules:
  0.0 129.3 jit_solution(13281405562622240602)
XLA Ops:
  0.0 2.5 %copy.9.cells = bf16[128,20,128]{2,1,0:T(8,128)(2,1)} copy(bf16[128,20,128]{2,0,1:T(8,128)(2,1)} %param.8) | data formatting | bytes 1310720 | tf_op args[0]
  2.5 76.2 %mix.1 = (bf16[16,5,32,128]{3,2,1,0:T(8,128)(2,1)}, bf16[16,5,64,128]{3,2,1,0:T(8,128)(2,1)}) custom-call(bf16[128,20,128]{2,1,0:T(8,128)(2,1)} %copy.9.cells, s32[64]{0:T(128)} %table.3, s32[8192]{0:T(1024)} %live.1, s32[64,128]{1,0:T(8,128)} %bitcast.1, bf16[128,384]{1,0:T(8,128)(2,1)} %wqkv.2, bf16[128,128]{1,0:T(8,128)(2,1)} %wout.2), custom_call_target="tpu_custom_call" | custom-call | tf_op jit(solution)/shard_map/mix/pallas_call | solution.py:520
  78.7 35.2 %item.1.done = bf16[16,5,32,128]{3,2,1,0:T(8,128)(2,1)} custom-call(bf16[16,5,32,128]{3,2,1,0:T(8,128)(2,1)} %get-tuple-element.7.q_in, bf16[16,5,64,128]{3,2,1,0:T(8,128)(2,1)} %get-tuple-element.8.kv_in, s32[64]{0:T(128)} %table.3, s32[64,128]{1,0:T(8,128)} %bitcast.2, bf16[128,384]{1,0:T(8,128)(2,1)} %wqkv.3, bf16[128,128]{1,0:T(8,128)(2,1)} %wout.3), custom_call_target="tpu_custom_call" | custom-call | tf_op jit(solution)/shard_map/item/pallas_call | solution.py:547
  113.9 12.4 %back.1.rows = bf16[16,5,32,128]{3,2,1,0:T(8,128)(2,1)} custom-call(bf16[16,5,32,128]{3,2,1,0:T(8,128)(2,1)} %item.1.done), custom_call_target="tpu_custom_call" | custom-call | tf_op jit(solution)/shard_map/back/pallas_call | solution.py:560
  126.2 3.0 %turn.1 = bf16[32,80,128]{2,1,0:T(8,128)(2,1)} custom-call(bf16[16,5,32,128]{3,2,1,0:T(8,128)(2,1)} %back.1.rows), custom_call_target="tpu_custom_call" | custom-call | tf_op jit(solution)/shard_map/turn/pallas_call | solution.py:569
